TPU v7x, 256 devices: a whole 4x4x8 slice. The times are simulated.
256 devices in a mesh: narrow: 8 (over y, core), wide: 32 (over x, z).
Axes of the slice: x: 4, y: 4, z: 8, core: 2. Of those that a mesh axis runs over, the one named last changes fastest.
Arguments:
- points: float32 [2, 32768], P(None, ('narrow', 'wide')), may hold values from 0 to 1
- quad_weight: float32 [32768], P(('narrow', 'wide')), may hold values from 9.155274e-06 to 9.1552734e-05
- basis: float32 [4, 2, 32768, 128], P(None, None, ('narrow', 'wide')), may hold values from -6 to 6
- jacobi: float32 [2, 32768], P(None, ('narrow', 'wide')), may hold values from 0.5 to 2
- near_panel: int32 [2048, 12], P(('narrow', 'wide')), may hold values from 0 to 2047, as said below
- near_count: int32 [2048], P(('narrow', 'wide')), may hold values from 2 to 12, as said below
- near_block: bfloat16 [2048, 12, 32, 32], P(('narrow', 'wide')), may hold values from -0.875 to 0.875
- agg_index: int32 [2, 32768], P(None, ('narrow', 'wide')), may hold values from 0 to 47
- coarse_inverse: float32 [8, 1536, 12288], P(None, 'wide', 'narrow'), may hold values from -0.1 to 0.5
Outputs:
- new_block: float32 [2, 32768, 128], P(None, ('narrow', 'wide'))
- hessenberg: float32 [4, 128, 128], replicated
- upper_factor: float32 [128, 128], replicated
Inputs may be any that keep to these rules, and one draw needn't show every extreme that they name: near_panel[p, 0] = p; every entry lies within 4 panels of p in panel order, and some entry lies exactly 4 panels away. `near_count`: slots at or beyond a panel's count are not used; some panel uses all 12.
All inputs are finite; a program needn't handle non-finite values.
Results may differ from a plain program's by a relative error of at most 0.0027.
The roundings to bfloat16 on the way count: a program that leaves them out, or rounds other values in their place, can miss the bound.
Values may be sent and summed in bfloat16 or wider, within the bound.
A program may use at most 64 MiB of HBM per device.

v0:
```python
import math
import jax
import jax.numpy as jnp
from jax import lax
from jax.sharding import PartitionSpec as P

SPAN = 4
NU = 0.3
DELTA2 = 1e-05
ELASTIC = 40.0
HIGH = lax.Precision.HIGHEST


def extended(block, sides, width):
    for axis, dim in sides:
        count = lax.axis_size(axis)
        forward = [(i, i + 1) for i in range(count - 1)]
        backward = [(target, source) for source, target in forward]
        low = lax.ppermute(
            lax.slice_in_dim(block, block.shape[dim] - width, None, axis=dim), axis, forward
        )
        high = lax.ppermute(lax.slice_in_dim(block, 0, width, axis=dim), axis, backward)
        block = jnp.concatenate([low, block, high], axis=dim)
    return block


def far_kernel(targets, sources, weights):
    delta_x = targets[0][:, None] - sources[0][None, :]
    delta_y = targets[1][:, None] - sources[1][None, :]
    square_dist = delta_x * delta_x + delta_y * delta_y + DELTA2
    factor = ELASTIC * weights[None, :]
    log_part = -0.5 * (3.0 - 4.0 * NU) * jnp.log(square_dist)
    g_xx = factor * (log_part + delta_x * delta_x / square_dist)
    g_xy = factor * (delta_x * delta_y / square_dist)
    g_yy = factor * (log_part + delta_y * delta_y / square_dist)
    first_row = jnp.stack([g_xx, g_xy], axis=1)
    second_row = jnp.stack([g_xy, g_yy], axis=1)
    stacked = jnp.stack([first_row, second_row], axis=0)
    return stacked.reshape(2 * targets.shape[1], 2 * sources.shape[1]).astype(jnp.bfloat16)


def far_product(targets, sources, weights, fields):
    piece_len = sources.shape[1]
    row_count = targets.shape[1]
    rhs_count = fields.shape[2]
    block_size = math.gcd(piece_len, max(512, 524288 // row_count))
    block_count = piece_len // block_size

    def one_block(block_index, running):
        offset = block_index * block_size
        source_block = lax.dynamic_slice_in_dim(sources, offset, block_size, 1)
        weight_block = lax.dynamic_slice_in_dim(weights, offset, block_size, 0)
        field_block = lax.dynamic_slice_in_dim(fields, offset, block_size, 1)
        kernel_block = far_kernel(targets, source_block, weight_block)
        return running + jnp.dot(
            kernel_block,
            field_block.reshape(2 * block_size, rhs_count),
            preferred_element_type=jnp.float32,
        )

    initial = jnp.zeros((2 * row_count, rhs_count), jnp.float32)
    return lax.fori_loop(0, block_count, one_block, initial)


def make_fold(targets, source_all, shard_piece):
    return far_product(targets, source_all[0:2], source_all[2], shard_piece)


def body(
    points,
    quad_weight,
    basis,
    jacobi,
    near_panel,
    near_count,
    near_block,
    agg_index,
    coarse_inverse,
):
    block_total = basis.shape[0]
    point_count = basis.shape[2]
    rhs_count = basis.shape[3]
    coarse_count = coarse_inverse.shape[1]
    newest = basis[block_total - 1]
    member = (
        agg_index[:, :, None] == jnp.arange(coarse_count, dtype=jnp.int32)[None, None, :]
    ).astype(jnp.float32)
    coarse_rhs = jnp.einsum("apc,apr->cr", member, newest, precision=HIGH)
    coarse_part = jnp.einsum(
        "abc,cr->abr",
        coarse_inverse,
        lax.all_gather(coarse_rhs, "wide", axis=0, tiled=True),
        precision=HIGH,
    )
    coarse_sol = lax.psum_scatter(coarse_part, "narrow", scatter_dimension=0, tiled=True)[0]
    lifted = jnp.einsum("apc,cr->apr", member, coarse_sol, precision=HIGH)
    precond = (jacobi[:, :, None] * newest + lifted).astype(jnp.bfloat16)
    source_info = jnp.concatenate([points, quad_weight[None, :]], axis=0)
    targets = lax.all_gather(points, "narrow", axis=1, tiled=True)
    source_all = lax.all_gather(source_info, "wide", axis=1, tiled=True)
    far_part = make_fold(targets, source_all, lax.all_gather(precond, "wide", axis=1, tiled=True))
    far_local = lax.psum_scatter(
        far_part.reshape(2, targets.shape[1], rhs_count), "narrow", scatter_dimension=1, tiled=True
    )
    panels_dev = near_panel.shape[0]
    slot_total = near_panel.shape[1]
    nodes = near_block.shape[2] // 2
    padded = extended(precond, ((("narrow", "wide"), 1),), SPAN * nodes)
    panel_fields = padded.reshape(2, panels_dev + 2 * SPAN, nodes, rhs_count)
    local_index = near_panel - lax.axis_index(("narrow", "wide")) * panels_dev + SPAN
    gathered = panel_fields[:, local_index]
    slot_live = jnp.arange(slot_total, dtype=jnp.int32)[None, :] < near_count[:, None]
    gathered = jnp.where(slot_live[None, :, :, None, None], gathered, jnp.zeros((), gathered.dtype))
    gathered = jnp.transpose(gathered, (1, 2, 0, 3, 4)).reshape(
        panels_dev, slot_total, 2 * nodes, rhs_count
    )
    near_terms = jnp.einsum(
        "pkxy,pkyr->pxr", near_block, gathered, preferred_element_type=jnp.float32
    )
    near = jnp.transpose(near_terms.reshape(panels_dev, 2, nodes, rhs_count), (1, 0, 2, 3)).reshape(
        2, point_count, rhs_count
    )
    image = 0.5 * precond.astype(jnp.float32) + far_local + near
    weighted = basis * quad_weight[None, None, :, None]
    local_proj = jnp.einsum("jair,aiw->jrw", weighted, image, precision=HIGH)
    hessenberg = lax.psum(local_proj, ("narrow", "wide"))
    remainder = image - jnp.einsum("jair,jrw->aiw", basis, hessenberg, precision=HIGH)
    local_gram = jnp.einsum(
        "air,aiw->rw", remainder * quad_weight[None, :, None], remainder, precision=HIGH
    )
    gram_matrix = lax.psum(local_gram, ("narrow", "wide"))
    lower_factor = jnp.linalg.cholesky(gram_matrix)
    flat = remainder.reshape(2 * point_count, rhs_count)
    solved = jax.scipy.linalg.solve_triangular(lower_factor, flat.T, lower=True)
    new_block = solved.T.reshape(2, point_count, rhs_count)
    return (new_block, hessenberg, lower_factor.T)


def solution(mesh):
    in_specs = (
        P(None, ("narrow", "wide")),
        P(("narrow", "wide")),
        P(None, None, ("narrow", "wide"), None),
        P(None, ("narrow", "wide")),
        P(("narrow", "wide"), None),
        P(("narrow", "wide")),
        P(("narrow", "wide"), None, None, None),
        P(None, ("narrow", "wide")),
        P(None, "wide", "narrow"),
    )
    out_specs = (P(None, ("narrow", "wide"), None), P(), P())
    return jax.shard_map(body, mesh=mesh, in_specs=in_specs, out_specs=out_specs, check_vma=False)
```

profile of v0, /device:TPU:1, one launch (start us, length us, event | category | flops | bytes accessed | tf_op | source)
XLA Modules:
  0.0 911.1 jit_solution(4539948616988339396)
XLA Ops:
  7.2 1.2 convolution_bitcast_fusion.4
  8.5 42.3 %all_gather.12 = f32[1536,128]{1,0:T(8,128)S(1)} all-gather(f32[48,128]{1,0:T(8,128)S(1)} %convolution_bitcast_fusion.4), channel_id=1, replica_groups=mesh['narrow'=8,'wide'=32] {'wide'}, dimensions={0}, use_global_device_ids=true | all-gather | bytes 811008 | tf_op jit(solution)/shard_map/all_gather | solution.py:92
  50.9 2.7 convolution_bitcast_fusion.1
  53.6 40.3 %reduce-scatter.3.cloned.1.call-done = f32[1,48,128]{2,1,0:T(8,128)} async-done(((f32[8,48,128]{2,1,0:T(8,128)}), f32[1,48,128]{2,1,0:T(8,128)}) %reduce-scatter.3.cloned.1.call-update) | async-done | bytes 24592 | tf_op jit(solution)/shard_map/reduce_scatter | solution.py:95
  94.0 1.8 fusion.16
  95.9 38.2 %all_gather.13 = f32[3,4096]{1,0:T(4,128)S(1)} all-gather(f32[3,128]{1,0:T(4,128)S(1)} %pad_maximum_fusion.2), channel_id=1, replica_groups=mesh['narrow'=8,'wide'=32] {'wide'}, dimensions={1}, use_global_device_ids=true | all-gather | bytes 50688 | tf_op jit(solution)/shard_map/all_gather | solution.py:100
  134.2 22.4 %all_gather.14 = f32[2,1024]{1,0:T(2,128)S(1)} all-gather(f32[2,128]{1,0:T(2,128)S(1)} %copy-done.8), channel_id=1, replica_groups=mesh['narrow'=8,'wide'=32] {'narrow'}, dimensions={1}, use_global_device_ids=true | all-gather | bytes 9216 | tf_op jit(solution)/shard_map/all_gather | solution.py:99
  156.6 14.8 %all-gather.2.cloned.1.call-done = bf16[2,4096,128]{2,1,0:T(8,128)(2,1)} async-done(((bf16[2,128,128]{2,1,0:T(8,128)(2,1)}), bf16[2,4096,128]{2,1,0:T(8,128)(2,1)}) %all-gather.2.cloned.1.call-update) | async-done | bytes 2097168 | tf_op jit(solution)/shard_map/all_gather | solution.py:101
  171.5 163.6 %while.14 = (s32[]{:T(128)}, f32[2048,128]{1,0:T(8,128)}, f32[4096]{0:T(1024)S(1)}, f32[2,1024]{1,0:T(2,128)S(1)}, f32[2,4096]{1,0:T(2,128)S(1)}, /*index=5*/bf1...) while((s32[]{:T(128)}, f32[2048,128]{1,0:T(8,128)}, ...), condition=%wide.region_2.0_spmd.clone, body=%wide.region_1.0_spmd.clone.sunk | while | flops 551551488 | bytes 51161332 | solution.py:62
  171.6 1.6 fusion.51
  174.0 6.3 copy.58
  180.3 5.4 copy.59
  185.7 1.7 constant_dynamic-slice_fusion.5
  187.4 3.5 convolution_add_fusion.3
  192.1 1.6 fusion.51
  194.4 6.3 copy.58
  200.7 5.4 copy.59
  206.2 1.7 constant_dynamic-slice_fusion.5
  207.8 3.5 convolution_add_fusion.3
  212.5 1.6 fusion.51
  214.9 6.3 copy.58
  221.2 5.4 copy.59
  226.6 1.7 constant_dynamic-slice_fusion.5
  228.3 3.5 convolution_add_fusion.3
  233.0 1.6 fusion.51
  235.3 6.3 copy.58
  241.6 5.4 copy.59
  247.1 1.7 constant_dynamic-slice_fusion.5
  248.7 3.5 convolution_add_fusion.3
  252.3 1.0 copy-done.2
  253.4 1.6 fusion.51
  255.8 6.3 copy.58
  262.1 5.4 copy.59
  267.5 1.7 constant_dynamic-slice_fusion.5
  269.2 3.5 convolution_add_fusion.3
  273.9 1.6 fusion.51
  276.2 6.3 copy.58
  282.5 5.4 copy.59
  288.0 1.7 constant_dynamic-slice_fusion.5
  289.6 3.5 convolution_add_fusion.3
  294.3 1.6 fusion.51
  296.7 6.3 copy.58
  303.0 5.4 copy.59
  308.4 1.7 constant_dynamic-slice_fusion.5
  310.1 3.5 convolution_add_fusion.3
  314.8 1.6 fusion.51
  317.1 6.3 copy.58
  323.4 5.4 copy.59
  328.8 1.7 constant_dynamic-slice_fusion.5
  330.5 3.5 convolution_add_fusion.3
  335.3 2.4 collective-permute-start
  337.7 8.7 collective-permute-start.1
  346.4 1.0 collective-permute-done.1
  347.4 1.6 gather_fusion
  349.0 1.4 broadcast_select_fusion
  350.4 1.6 fusion.35
  352.0 17.6 %reduce-scatter.5.cloned.1.call-done = f32[2,128,128]{2,1,0:T(8,128)} async-done(((f32[2,1024,128]{2,1,0:T(8,128)}), f32[2,128,128]{2,1,0:T(8,128)}) %reduce-scatter.5.cloned.1.call-update) | async-done | bytes 131088 | tf_op jit(solution)/shard_map/reduce_scatter | solution.py:102
  370.6 1.8 convolution_bitcast_fusion
  372.6 256.9 %all-reduce.3.cloned.1.call-done = f32[4,128,128]{2,1,0:T(8,128)} async-done(((f32[4,128,128]{2,1,0:T(8,128)}), f32[4,128,128]{2,1,0:T(8,128)}) %all-reduce.3.cloned.1.call-update) | async-done | bytes 262160 | tf_op jit(solution)/shard_map/psum | solution.py:126
  629.5 1.6 fusion.15
  631.1 1.1 convolution_bitcast_fusion.3
  632.2 245.4 %all-reduce.5.cloned.1.call-done = f32[128,128]{0,1:T(8,128)} async-done(((f32[128,128]{0,1:T(8,128)}), f32[128,128]{0,1:T(8,128)}) %all-reduce.5.cloned.1.call-update) | async-done | bytes 65552 | tf_op jit(solution)/shard_map/psum | solution.py:131
  879.4 11.7 %cholesky.16 = f32[128,128]{1,0:T(8,128)S(1)} custom-call(f32[128,128]{1,0:T(8,128)S(1)} %fusion.27), custom_call_target="Cholesky" | custom-call | tf_op jit(solution)/shard_map/jit(cholesky)/cholesky | solution.py:132
  892.4 9.8 %custom-call.7 = f32[1,128,128]{1,2,0:T(8,128)S(1)} custom-call(f32[1,128,128]{2,1,0:T(8,128)S(1)} %get-tuple-element.165), custom_call_target="InvertDiagBlocksLowerTriangular" | custom-call | tf_op jit(solution)/shard_map/jit(_solve_triangular)/triangular_solve | solution.py:134
  (122 shorter events, 21.3 us)
Async XLA Ops:
  7.2 43.7 %copy-start = (f32[8,48,1536]{2,1,0:T(8,128)S(1)}, f32[8,48,1536]{2,1,0:T(8,128)}, u32[]{:S(2)}) copy-start(f32[8,48,1536]{2,1,0:T(8,128)} %param.19) | copy-start | bytes 7077892
  7.2 86.8 %reduce-scatter.3.cloned.1.call-start = ((), (), s32[]{:S(2)}) async-start(), calls=%async_computation.2 | async-start | bytes 221184 | tf_op jit(solution)/shard_map/reduce_scatter | solution.py:95
  8.5 85.5 %copy-start.7 = (s32[2,128]{1,0:T(2,128)S(1)}, s32[2,128]{1,0:T(2,128)}, u32[]{:S(2)}) copy-start(s32[2,128]{1,0:T(2,128)} %param.18) | copy-start | bytes 3076
  8.5 85.5 %copy-start.10 = (f32[2,128]{1,0:T(2,128)S(1)}, f32[2,128]{1,0:T(2,128)}, u32[]{:S(2)}) copy-start(f32[2,128]{1,0:T(2,128)} %param.14) | copy-start | bytes 3076
  50.9 45.1 %copy-start.6 = (f32[128]{0:T(128)S(1)}, f32[128]{0:T(128)}, u32[]{:S(2)}) copy-start(f32[128]{0:T(128)} %param.12) | copy-start | bytes 1540
  50.9 45.1 %copy-start.8 = (f32[2,128]{1,0:T(2,128)S(1)}, f32[2,128]{1,0:T(2,128)}, u32[]{:S(2)}) copy-start(f32[2,128]{1,0:T(2,128)} %param.11) | copy-start | bytes 3076
  53.6 117.9 %all-gather.2.cloned.1.call-start = ((), (), s32[]{:S(2)}) async-start(), calls=%async_computation.3 | async-start | bytes 2162688 | tf_op jit(solution)/shard_map/all_gather | solution.py:101
  95.9 273.8 %reduce-scatter.5.cloned.1.call-start = ((), (), s32[]{:S(2)}) async-start(), calls=%async_computation.4 | async-start | bytes 1179648 | tf_op jit(solution)/shard_map/reduce_scatter | solution.py:102
  171.5 163.7 %copy-start.9 = (s32[8,12]{1,0:T(8,128)S(1)}, s32[8,12]{1,0:T(8,128)}, u32[]{:S(2)}) copy-start(s32[8,12]{1,0:T(8,128)} %param.15) | copy-start | bytes 1156
  171.5 163.8 %copy-start.11 = (s32[8]{0:T(128)S(1)}, s32[8]{0:T(128)}, u32[]{:S(2)}) copy-start(s32[8]{0:T(128)} %param.16) | copy-start | bytes 100
  171.5 163.8 %copy-start.4 = (bf16[2,128,128]{2,1,0:T(8,128)(2,1)S(1)}, bf16[2,128,128]{2,1,0:T(8,128)(2,1)}, u32[]{:S(2)}) copy-start(bf16[2,128,128]{2,1,0:T(8,128)(2,1)} %fusion.16) | copy-start | bytes 196612
  180.3 7.1 copy-start.1
  190.9 1.0 copy-start.2
  200.7 7.1 copy-start.1
  211.4 1.0 copy-start.2
  221.2 7.1 copy-start.1
  231.8 1.0 copy-start.2
  241.6 7.1 copy-start.1
  252.3 1.0 copy-start.2
  262.1 7.1 copy-start.1
  272.7 1.0 copy-start.2
  282.5 7.1 copy-start.1
  293.2 1.0 copy-start.2
  303.0 7.1 copy-start.1
  313.6 1.0 copy-start.2
  323.4 7.1 copy-start.1
  334.1 1.0 copy-start.2
  335.1 294.4 %all-reduce.3.cloned.1.call-start = ((), (), s32[]{:S(2)}) async-start(), calls=%async_computation.5 | async-start | bytes 524288 | tf_op jit(solution)/shard_map/psum | solution.py:126
  335.3 11.1 %collective-permute-start = (bf16[2,64,128]{2,1,0:T(8,128)(2,1)S(1)}, bf16[2,64,128]{2,1,0:T(8,128)(2,1)S(1)}, u32[]{:S(2)}, u32[]{:S(2)}) collective-permute-start(bf16[2,64,128]{2,1,0:T(8,128)(2,1)S(1)} %get-tuple-element.166), channel_id=1, source_target_pairs={{0,1},{1,2},{2,3},{3,4},{4,5},{5,6},{6,7},{7,8},{8,9},{9,10},{10,1... | collective-permute-start | bytes 98312 | tf_op jit(solution)/shard_map/ppermute | solution.py:19
  337.7 9.7 %collective-permute-start.1 = (bf16[2,64,128]{2,1,0:T(8,128)(2,1)S(1)}, bf16[2,64,128]{2,1,0:T(8,128)(2,1)S(1)}, u32[]{:S(2)}, u32[]{:S(2)}) collective-permute-start(bf16[2,64,128]{2,1,0:T(8,128)(2,1)S(1)} %get-tuple-element.167), channel_id=1, source_target_pairs={{1,0},{2,1},{3,2},{4,3},{5,4},{6,5},{7,6},{8,7},{9,8},{10,9},{11,1... | collective-permute-start | bytes 98312 | tf_op jit(solution)/shard_map/ppermute | solution.py:22
  349.0 21.5 %copy-start.3 = (f32[4,2,128,128]{3,2,1,0:T(8,128)S(1)}, f32[4,2,128,128]{3,2,1,0:T(8,128)}, u32[]{:S(2)}) copy-start(f32[4,2,128,128]{3,2,1,0:T(8,128)} %param.13) | copy-start | bytes 1572868
  372.4 505.2 %all-reduce.5.cloned.1.call-start = ((), (), s32[]{:S(2)}) async-start(), calls=%async_computation.6 | async-start | bytes 131072 | tf_op jit(solution)/shard_map/psum | solution.py:131
  629.5 274.4 %copy-start.5 = (f32[4,128,128]{2,1,0:T(8,128)S(1)}, f32[4,128,128]{2,1,0:T(8,128)}, u32[]{:S(2)}) copy-start(f32[4,128,128]{2,1,0:T(8,128)} %all-reduce.3.cloned.1.call-done) | copy-start | bytes 786436
Sparse Core Ops, SparseCore 0:
  53.7 40.2 reduce-scatter.2
  97.1 74.2 all-gather.1
  335.2 34.3 reduce-scatter.4
  375.5 253.9 all-reduce.2
  635.4 242.0 all-reduce.4
where the time goes:
time: 912 us; the launch traced here: 911 us
  waiting for transfers between devices  576 us (63%)
  local copies, waits for them, and re-layouts  120 us (13%)
  blocking collectives  103 us (11%)
  other arithmetic  45.4 us (5%)
  matrix products  41.1 us (5%)
  between operations  14 us (2%)
  starting transfers between devices  11.5 us (1%)
    psum x1, waiting for transfers between devices, body(): hessenberg = lax.psum(local_proj, ('narrow', 'wide'))  257 us
    psum x1, waiting for transfers between devices, body(): gram_matrix = lax.psum(local_gram, ('narrow', 'wide'))  245 us
    while x40, local copies, waits for them, and re-layouts  51.2 us
    another operation x8, local copies, waits for them, and re-layouts, far_kernel(): stacked = jnp.stack([first_row, second_row], axis=0)  50.4 us
    all_gather x1, blocking collectives, body(): lax.all_gather(coarse_rhs, 'wide', axis=0, tiled=True)  42.3 us
    reduce_scatter x1, waiting for transfers between devices, body(): lax.psum_scatter(coarse_part, 'narrow', scatter_dimension=0, tiled=True)[0]  40.3 us
    all_gather x1, blocking collectives, body(): source_all = lax.all_gather(source_info, 'wide', axis=1, tiled=True)  38.2 us
    dot_general x8, matrix products, one_block(): jnp.dot(kernel_block, field_block.reshape(2 * block_size, rhs_count), pre...  28.3 us
  transfers between devices with their start and end apart: 7, of which 6 were waited for; matrix products, arithmetic and copies ran while one was open for 1% of the time, Pallas kernels for 0%

commit v1 on v0

--- a/solution.py
+++ b/solution.py
@@ -123,7 +123,9 @@
     image = 0.5 * precond.astype(jnp.float32) + far_local + near
     weighted = basis * quad_weight[None, None, :, None]
     local_proj = jnp.einsum("jair,aiw->jrw", weighted, image, precision=HIGH)
-    hessenberg = lax.psum(local_proj, ("narrow", "wide"))
+    hessenberg = local_proj
+    for mesh_axis in ("wide", "narrow"):
+        hessenberg = lax.psum(hessenberg, mesh_axis)
     remainder = image - jnp.einsum("jair,jrw->aiw", basis, hessenberg, precision=HIGH)
     local_gram = jnp.einsum(
         "air,aiw->rw", remainder * quad_weight[None, :, None], remainder, precision=HIGH

time: 912 us -> 866 us (0.950)
  waiting for transfers between devices: 576 us -> 530 us
    psum x1 -> x2, waiting for transfers between devices: 257 us -> 210 us  [body(): hessenberg = lax.psum(hessenberg, mesh_axis)]
  transfers between devices with their start and end apart: 7 -> 8, of which waited for: 6 -> 7; matrix products, arithmetic and copies ran while one was open for 1% -> 1% of each run, Pallas kernels for 0% -> 0%
where the time goes in v1:
time: 866 us
  waiting for transfers between devices  530 us (61%)
  local copies, waits for them, and re-layouts  120 us (14%)
  blocking collectives  103 us (12%)
  other arithmetic  45.4 us (5%)
  matrix products  41.1 us (5%)
  between operations  14.3 us (2%)
  starting transfers between devices  11.5 us (1%)
    psum x1, waiting for transfers between devices, body(): gram_matrix = lax.psum(local_gram, ('narrow', 'wide'))  246 us
    psum x2, waiting for transfers between devices, body(): hessenberg = lax.psum(hessenberg, mesh_axis)  210 us
    while x40, local copies, waits for them, and re-layouts  51.2 us
    another operation x8, local copies, waits for them, and re-layouts, far_kernel(): stacked = jnp.stack([first_row, second_row], axis=0)  50.4 us
    all_gather x1, blocking collectives, body(): lax.all_gather(coarse_rhs, 'wide', axis=0, tiled=True)  42.3 us
    reduce_scatter x1, waiting for transfers between devices, body(): lax.psum_scatter(coarse_part, 'narrow', scatter_dimension=0, tiled=True)[0]  40.3 us
    all_gather x1, blocking collectives, body(): source_all = lax.all_gather(source_info, 'wide', axis=1, tiled=True)  38.2 us
    dot_general x8, matrix products, one_block(): jnp.dot(kernel_block, field_block.reshape(2 * block_size, rhs_count), pre...  28.3 us
  transfers between devices with their start and end apart: 8, of which 7 were waited for; matrix products, arithmetic and copies ran while one was open for 1% of the time, Pallas kernels for 0%

profile of v1, /device:TPU:1, one launch (start us, length us, event | category | flops | bytes accessed | tf_op | source)
XLA Modules:
  0.0 865.6 jit_solution(3469910481630057955)
XLA Ops:
  7.2 1.2 convolution_bitcast_fusion.4
  8.5 42.3 %all_gather.12 = f32[1536,128]{1,0:T(8,128)S(1)} all-gather(f32[48,128]{1,0:T(8,128)S(1)} %convolution_bitcast_fusion.4), channel_id=1, replica_groups=mesh['narrow'=8,'wide'=32] {'wide'}, dimensions={0}, use_global_device_ids=true | all-gather | bytes 811008 | tf_op jit(solution)/shard_map/all_gather | solution.py:92
  50.9 2.7 convolution_bitcast_fusion.1
  53.6 40.3 %reduce-scatter.3.cloned.1.call-done = f32[1,48,128]{2,1,0:T(8,128)} async-done(((f32[8,48,128]{2,1,0:T(8,128)}), f32[1,48,128]{2,1,0:T(8,128)}) %reduce-scatter.3.cloned.1.call-update) | async-done | bytes 24592 | tf_op jit(solution)/shard_map/reduce_scatter | solution.py:95
  94.0 1.8 fusion.16
  95.9 38.2 %all_gather.13 = f32[3,4096]{1,0:T(4,128)S(1)} all-gather(f32[3,128]{1,0:T(4,128)S(1)} %pad_maximum_fusion.2), channel_id=1, replica_groups=mesh['narrow'=8,'wide'=32] {'wide'}, dimensions={1}, use_global_device_ids=true | all-gather | bytes 50688 | tf_op jit(solution)/shard_map/all_gather | solution.py:100
  134.2 22.4 %all_gather.14 = f32[2,1024]{1,0:T(2,128)S(1)} all-gather(f32[2,128]{1,0:T(2,128)S(1)} %copy-done.8), channel_id=1, replica_groups=mesh['narrow'=8,'wide'=32] {'narrow'}, dimensions={1}, use_global_device_ids=true | all-gather | bytes 9216 | tf_op jit(solution)/shard_map/all_gather | solution.py:99
  156.6 14.8 %all-gather.2.cloned.1.call-done = bf16[2,4096,128]{2,1,0:T(8,128)(2,1)} async-done(((bf16[2,128,128]{2,1,0:T(8,128)(2,1)}), bf16[2,4096,128]{2,1,0:T(8,128)(2,1)}) %all-gather.2.cloned.1.call-update) | async-done | bytes 2097168 | tf_op jit(solution)/shard_map/all_gather | solution.py:101
  171.5 163.6 %while.14 = (s32[]{:T(128)}, f32[2048,128]{1,0:T(8,128)}, f32[4096]{0:T(1024)S(1)}, f32[2,1024]{1,0:T(2,128)S(1)}, f32[2,4096]{1,0:T(2,128)S(1)}, /*index=5*/bf1...) while((s32[]{:T(128)}, f32[2048,128]{1,0:T(8,128)}, ...), condition=%wide.region_2.0_spmd.clone, body=%wide.region_1.0_spmd.clone.sunk | while | flops 551551488 | bytes 51161332 | solution.py:62
  171.6 1.6 fusion.51
  174.0 6.3 copy.58
  180.3 5.4 copy.59
  185.7 1.7 constant_dynamic-slice_fusion.5
  187.4 3.5 convolution_add_fusion.3
  192.1 1.6 fusion.51
  194.4 6.3 copy.58
  200.7 5.4 copy.59
  206.2 1.7 constant_dynamic-slice_fusion.5
  207.8 3.5 convolution_add_fusion.3
  212.5 1.6 fusion.51
  214.9 6.3 copy.58
  221.2 5.4 copy.59
  226.6 1.7 constant_dynamic-slice_fusion.5
  228.3 3.5 convolution_add_fusion.3
  233.0 1.6 fusion.51
  235.3 6.3 copy.58
  241.6 5.4 copy.59
  247.1 1.7 constant_dynamic-slice_fusion.5
  248.7 3.5 convolution_add_fusion.3
  253.4 1.6 fusion.51
  255.8 6.3 copy.58
  262.1 5.4 copy.59
  267.5 1.7 constant_dynamic-slice_fusion.5
  269.2 3.5 convolution_add_fusion.3
  273.9 1.6 fusion.51
  276.2 6.3 copy.58
  282.5 5.4 copy.59
  288.0 1.7 constant_dynamic-slice_fusion.5
  289.6 3.5 convolution_add_fusion.3
  294.3 1.6 fusion.51
  296.7 6.3 copy.58
  303.0 5.4 copy.59
  308.4 1.7 constant_dynamic-slice_fusion.5
  310.1 3.5 convolution_add_fusion.3
  314.8 1.6 fusion.51
  317.1 6.3 copy.58
  323.4 5.4 copy.59
  328.8 1.7 constant_dynamic-slice_fusion.5
  330.5 3.5 convolution_add_fusion.3
  335.3 2.4 collective-permute-start
  337.7 8.7 %collective-permute-start.1 = (bf16[2,64,128]{2,1,0:T(8,128)(2,1)S(1)}, bf16[2,64,128]{2,1,0:T(8,128)(2,1)S(1)}, u32[]{:S(2)}, u32[]{:S(2)}) collective-permute-start(bf16[2,64,128]{2,1,0:T(8,128)(2,1)S(1)} %get-tuple-element.167), channel_id=1, source_target_pairs={{1,0},{2,1},{3,2},{4,3},{5,4},{6,5},{7,6},{8,7},{9,8},{10,9},{11,1... | collective-permute-start | bytes 98312 | tf_op jit(solution)/shard_map/ppermute | solution.py:22
  346.4 1.0 collective-permute-done.1
  347.4 1.6 gather_fusion
  349.0 1.4 broadcast_select_fusion
  350.4 1.6 fusion.35
  352.0 17.6 %reduce-scatter.5.cloned.1.call-done = f32[2,128,128]{2,1,0:T(8,128)} async-done(((f32[2,1024,128]{2,1,0:T(8,128)}), f32[2,128,128]{2,1,0:T(8,128)}) %reduce-scatter.5.cloned.1.call-update) | async-done | bytes 131088 | tf_op jit(solution)/shard_map/reduce_scatter | solution.py:102
  370.6 1.8 convolution_bitcast_fusion
  372.4 143.5 %all-reduce.4.cloned.1.call-done = f32[4,128,128]{2,1,0:T(8,128)} async-done(((f32[4,128,128]{2,1,0:T(8,128)}), f32[4,128,128]{2,1,0:T(8,128)}) %all-reduce.4.cloned.1.call-update) | async-done | bytes 262160 | tf_op jit(solution)/shard_map/psum | solution.py:128
  516.2 66.7 %all-reduce.6.cloned.1.call-done = f32[4,128,128]{2,1,0:T(8,128)} async-done(((f32[4,128,128]{2,1,0:T(8,128)}), f32[4,128,128]{2,1,0:T(8,128)}) %all-reduce.6.cloned.1.call-update) | async-done | bytes 262160 | tf_op jit(solution)/shard_map/psum | solution.py:128
  582.8 1.6 fusion.15
  584.4 1.1 convolution_bitcast_fusion.3
  585.5 246.2 %all-reduce.8.cloned.1.call-done = f32[128,128]{0,1:T(8,128)} async-done(((f32[128,128]{0,1:T(8,128)}), f32[128,128]{0,1:T(8,128)}) %all-reduce.8.cloned.1.call-update) | async-done | bytes 65552 | tf_op jit(solution)/shard_map/psum | solution.py:133
  833.6 11.7 %cholesky.16 = f32[128,128]{1,0:T(8,128)S(1)} custom-call(f32[128,128]{1,0:T(8,128)S(1)} %fusion.27), custom_call_target="Cholesky" | custom-call | tf_op jit(solution)/shard_map/jit(cholesky)/cholesky | solution.py:134
  846.6 9.8 %custom-call.7 = f32[1,128,128]{1,2,0:T(8,128)S(1)} custom-call(f32[1,128,128]{2,1,0:T(8,128)S(1)} %get-tuple-element.165), custom_call_target="InvertDiagBlocksLowerTriangular" | custom-call | tf_op jit(solution)/shard_map/jit(_solve_triangular)/triangular_solve | solution.py:136
  (125 shorter events, 22.3 us)
Async XLA Ops:
  7.2 43.7 %copy-start = (f32[8,48,1536]{2,1,0:T(8,128)S(1)}, f32[8,48,1536]{2,1,0:T(8,128)}, u32[]{:S(2)}) copy-start(f32[8,48,1536]{2,1,0:T(8,128)} %param.19) | copy-start | bytes 7077892
  7.2 86.8 %reduce-scatter.3.cloned.1.call-start = ((), (), s32[]{:S(2)}) async-start(), calls=%async_computation.2 | async-start | bytes 221184 | tf_op jit(solution)/shard_map/reduce_scatter | solution.py:95
  8.5 85.5 %copy-start.7 = (s32[2,128]{1,0:T(2,128)S(1)}, s32[2,128]{1,0:T(2,128)}, u32[]{:S(2)}) copy-start(s32[2,128]{1,0:T(2,128)} %param.18) | copy-start | bytes 3076
  8.5 85.5 %copy-start.10 = (f32[2,128]{1,0:T(2,128)S(1)}, f32[2,128]{1,0:T(2,128)}, u32[]{:S(2)}) copy-start(f32[2,128]{1,0:T(2,128)} %param.14) | copy-start | bytes 3076
  50.9 45.1 %copy-start.6 = (f32[128]{0:T(128)S(1)}, f32[128]{0:T(128)}, u32[]{:S(2)}) copy-start(f32[128]{0:T(128)} %param.12) | copy-start | bytes 1540
  50.9 45.1 %copy-start.8 = (f32[2,128]{1,0:T(2,128)S(1)}, f32[2,128]{1,0:T(2,128)}, u32[]{:S(2)}) copy-start(f32[2,128]{1,0:T(2,128)} %param.11) | copy-start | bytes 3076
  53.6 117.9 %all-gather.2.cloned.1.call-start = ((), (), s32[]{:S(2)}) async-start(), calls=%async_computation.3 | async-start | bytes 2162688 | tf_op jit(solution)/shard_map/all_gather | solution.py:101
  95.9 273.8 %reduce-scatter.5.cloned.1.call-start = ((), (), s32[]{:S(2)}) async-start(), calls=%async_computation.4 | async-start | bytes 1179648 | tf_op jit(solution)/shard_map/reduce_scatter | solution.py:102
  171.5 163.7 %copy-start.9 = (s32[8,12]{1,0:T(8,128)S(1)}, s32[8,12]{1,0:T(8,128)}, u32[]{:S(2)}) copy-start(s32[8,12]{1,0:T(8,128)} %param.15) | copy-start | bytes 1156
  171.5 163.8 %copy-start.11 = (s32[8]{0:T(128)S(1)}, s32[8]{0:T(128)}, u32[]{:S(2)}) copy-start(s32[8]{0:T(128)} %param.16) | copy-start | bytes 100
  171.5 163.8 %copy-start.4 = (bf16[2,128,128]{2,1,0:T(8,128)(2,1)S(1)}, bf16[2,128,128]{2,1,0:T(8,128)(2,1)}, u32[]{:S(2)}) copy-start(bf16[2,128,128]{2,1,0:T(8,128)(2,1)} %fusion.16) | copy-start | bytes 196612
  180.3 7.1 copy-start.1
  190.9 1.0 copy-start.2
  200.7 7.1 copy-start.1
  211.4 1.0 copy-start.2
  221.2 7.1 copy-start.1
  231.8 1.0 copy-start.2
  241.6 7.1 copy-start.1
  252.3 1.0 copy-start.2
  262.1 7.1 copy-start.1
  272.7 1.0 copy-start.2
  282.5 7.1 copy-start.1
  293.2 1.0 copy-start.2
  303.0 7.1 copy-start.1
  313.6 1.0 copy-start.2
  323.4 7.1 copy-start.1
  334.1 1.0 copy-start.2
  335.1 180.8 %all-reduce.4.cloned.1.call-start = ((), (), s32[]{:S(2)}) async-start(), calls=%async_computation.5 | async-start | bytes 524288 | tf_op jit(solution)/shard_map/psum | solution.py:128
  335.3 11.1 %collective-permute-start = (bf16[2,64,128]{2,1,0:T(8,128)(2,1)S(1)}, bf16[2,64,128]{2,1,0:T(8,128)(2,1)S(1)}, u32[]{:S(2)}, u32[]{:S(2)}) collective-permute-start(bf16[2,64,128]{2,1,0:T(8,128)(2,1)S(1)} %get-tuple-element.166), channel_id=1, source_target_pairs={{0,1},{1,2},{2,3},{3,4},{4,5},{5,6},{6,7},{7,8},{8,9},{9,10},{10,1... | collective-permute-start | bytes 98312 | tf_op jit(solution)/shard_map/ppermute | solution.py:19
  337.7 9.7 %collective-permute-start.1 = (bf16[2,64,128]{2,1,0:T(8,128)(2,1)S(1)}, bf16[2,64,128]{2,1,0:T(8,128)(2,1)S(1)}, u32[]{:S(2)}, u32[]{:S(2)}) collective-permute-start(bf16[2,64,128]{2,1,0:T(8,128)(2,1)S(1)} %get-tuple-element.167), channel_id=1, source_target_pairs={{1,0},{2,1},{3,2},{4,3},{5,4},{6,5},{7,6},{8,7},{9,8},{10,9},{11,1... | collective-permute-start | bytes 98312 | tf_op jit(solution)/shard_map/ppermute | solution.py:22
  349.0 21.5 %copy-start.3 = (f32[4,2,128,128]{3,2,1,0:T(8,128)S(1)}, f32[4,2,128,128]{3,2,1,0:T(8,128)}, u32[]{:S(2)}) copy-start(f32[4,2,128,128]{3,2,1,0:T(8,128)} %param.13) | copy-start | bytes 1572868
  372.4 210.5 %all-reduce.6.cloned.1.call-start = ((), (), s32[]{:S(2)}) async-start(), calls=%async_computation.6 | async-start | bytes 524288 | tf_op jit(solution)/shard_map/psum | solution.py:128
  515.9 315.9 %all-reduce.8.cloned.1.call-start = ((), (), s32[]{:S(2)}) async-start(), calls=%async_computation.7 | async-start | bytes 131072 | tf_op jit(solution)/shard_map/psum | solution.py:133
  582.8 275.3 %copy-start.5 = (f32[4,128,128]{2,1,0:T(8,128)S(1)}, f32[4,128,128]{2,1,0:T(8,128)}, u32[]{:S(2)}) copy-start(f32[4,128,128]{2,1,0:T(8,128)} %all-reduce.6.cloned.1.call-done) | copy-start | bytes 786436
Sparse Core Ops, SparseCore 0:
  53.7 40.2 reduce-scatter.2
  97.1 74.2 all-gather.1
  335.2 34.3 reduce-scatter.4
  373.5 142.3 all-reduce.3
  518.0 64.7 all-reduce.5
  588.8 242.9 all-reduce.7
